TPU v7x, 32 devices: a whole 2x2x4 slice. The times are simulated.
32 devices in a mesh: expert: 16 (over z, x, core), tensor: 2 (over y).
Axes of the slice: x: 2, y: 2, z: 4, core: 2. Of those that a mesh axis runs over, the one named last changes fastest.
Arguments:
- grad_out: bfloat16 [2048, 4096], P('expert', 'tensor'), may hold values from -1 to 1
- routes: int32 [2048, 6], P('expert'), may hold values from 0 to 15, all different within a row; in each aligned block of 128 rows (0 to 127, 128 to 255, ...) at most 96 rows name the same one
- scores: float32 [2048, 6], P('expert'), may hold values from -6 to 6
- hidden_act: bfloat16 [16, 1536, 1408], P('expert', None, 'tensor'), may hold values from -6 to 6
- w_down: bfloat16 [16, 1408, 4096], P('expert', 'tensor'), may hold values from -0.15625 to 0.15625
Outputs:
- d_hidden: bfloat16 [16, 1536, 1408], P('expert', None, 'tensor')
- grad_w: bfloat16 [16, 1408, 4096], P('expert', 'tensor')
- grad_scores: float32 [2048, 6], P('expert')
Inputs may be any that keep to these rules, and one draw needn't show every extreme that they name: `routes`: each row names 6 different experts. In each aligned block of 128 rows no expert is named by more than 96 rows, a bound that some block reaches.
All inputs are finite; a program needn't handle non-finite values.
Results may differ from a plain program's by a relative error of at most 0.012.
Values may be sent and summed in bfloat16 or wider, within the bound.
A program may use at most 128 MiB of HBM per device.

v0:
```python
import jax
import jax.numpy as jnp
from jax import lax
from jax.sharding import PartitionSpec as P


def shards(grad_out, routes, scores, hidden_act, w_down):
    expert_count = lax.axis_size("expert")
    tok_rows = routes.shape[0]
    top_count = routes.shape[1]
    slot_count = hidden_act.shape[1]
    per_source = slot_count // expert_count
    flat_routes = routes.reshape(-1)
    onehot = (flat_routes[:, None] == jnp.arange(expert_count, dtype=jnp.int32)[None, :]).astype(
        jnp.int32
    )
    slot_rank = jnp.sum((jnp.cumsum(onehot, axis=0) - onehot) * onehot, axis=1)
    slot_place = flat_routes * per_source + slot_rank
    gates = jax.nn.sigmoid(scores)
    gate_sum = jnp.sum(gates, axis=1, keepdims=True)
    probs = gates / gate_sum
    token_ids = jnp.arange(tok_rows * top_count, dtype=jnp.int32) // top_count
    slot_owner = (
        jnp.full((expert_count * per_source,), tok_rows, jnp.int32).at[slot_place].set(token_ids)
    )
    slot_probs = (
        jnp.zeros((expert_count * per_source,), jnp.float32).at[slot_place].set(probs.reshape(-1))
    )
    saved_act = hidden_act[0]
    down_rows = w_down[0]
    outgoing = jnp.take(grad_out, slot_owner, axis=0, mode="fill", fill_value=0).reshape(
        expert_count, per_source, -1
    )
    narrow, slot_weight = (
        lax.all_to_all(outgoing, "expert", split_axis=0, concat_axis=0, tiled=True),
        lax.all_to_all(
            slot_probs.reshape(expert_count, per_source).astype(jnp.bfloat16),
            "expert",
            split_axis=0,
            concat_axis=0,
            tiled=True,
        ).astype(jnp.float32),
    )
    narrow = narrow.reshape(slot_count, -1)
    slot_weight = slot_weight.reshape(slot_count)
    segment = lax.all_gather(narrow, "tensor", axis=1, tiled=True)
    proj_sum = lax.dot_general(
        segment, down_rows, (((1,), (1,)), ((), ())), preferred_element_type=jnp.float32
    )
    scaled = (segment * slot_weight[:, None]).astype(jnp.bfloat16)
    fresh = lax.dot_general(
        saved_act, scaled, (((0,), (0,)), ((), ())), preferred_element_type=jnp.float32
    )
    partial_value = jnp.sum(proj_sum * saved_act.astype(jnp.float32), axis=1)
    hidden_grad = (slot_weight[:, None] * proj_sum).astype(jnp.bfloat16)
    summed = lax.psum(partial_value, "tensor")
    returned = lax.all_to_all(
        summed.reshape(expert_count, per_source), "expert", split_axis=0, concat_axis=0, tiled=True
    )
    prob_grad = returned.reshape(-1)[slot_place].reshape(tok_rows, top_count)
    mean_term = jnp.sum(probs * prob_grad, axis=1, keepdims=True)
    grad_scores = gates * (1.0 - gates) * (prob_grad - mean_term) / gate_sum
    return (hidden_grad[None], fresh.astype(jnp.bfloat16)[None], grad_scores)


def solution(mesh):
    return jax.shard_map(
        shards,
        mesh=mesh,
        in_specs=(
            P("expert", "tensor"),
            P("expert", None),
            P("expert", None),
            P("expert", None, "tensor"),
            P("expert", "tensor", None),
        ),
        out_specs=(P("expert", None, "tensor"), P("expert", "tensor", None), P("expert", None)),
        check_vma=False,
    )
```

profile of v0, /device:TPU:0, one launch (start us, length us, event | category | flops | bytes accessed | tf_op | source)
XLA Modules:
  0.0 401.2 jit_solution(332698810590436367)
XLA Ops:
  7.2 0.0 copy-start
  7.2 0.0 all-gather.2.cloned.1.call-start
  7.2 0.8 copy.22
  8.1 0.1 eq.29
  8.2 0.1 eq.25
  8.3 0.7 broadcast_multiply_fusion
  9.1 1.7 reduce-window.6
  10.8 0.3 slice_reduce_fusion
  11.1 0.1 copy.21
  11.2 0.1 mul.49
  11.3 0.1 fusion.10
  11.4 3.4 scatter_custom_fusion.1
  14.9 0.1 broadcast_in_dim.34
  15.0 0.0 copy-done
  15.0 7.1 %gather_fusion = bf16[1536,2048]{1,0:T(8,128)(2,1)} fusion(bf16[128,2048]{1,0:T(8,128)(2,1)S(1)} %copy-done, s32[2048]{0:T(1024)S(1)} %pad_clamp_fusion), kind=kCustom, calls=%fused_computation | custom fusion | bytes 12589056 | tf_op jit(solution)/shard_map/jit(_take)/gather | solution.py:31
  22.1 3.3 broadcast_select_fusion
  25.3 144.3 %all_to_all.20 = bf16[16,96,2048]{2,1,0:T(8,128)(2,1)} all-to-all(bf16[16,96,2048]{2,1,0:T(8,128)(2,1)S(1)} %broadcast_select_fusion), channel_id=1, replica_groups=mesh['expert'=16,'tensor'=2] {'expert'}, dimensions={0} | all-to-all | bytes 12582912 | tf_op jit(solution)/shard_map/all_to_all | solution.py:35
  169.7 0.0 copy-start.1
  169.7 0.0 copy-start.2
  169.7 0.0 all-gather.2.cloned.1.call-update
  169.7 0.7 copy-done.1
  170.4 152.9 %all-gather.2.cloned.1.call-done = bf16[1536,4096]{1,0:T(8,128)(2,1)} async-done(((bf16[1536,2048]{1,0:T(8,128)(2,1)}), bf16[1536,4096]{1,0:T(8,128)(2,1)}) %all-gather.2.cloned.1.call-update) | async-done | bytes 12582928 | tf_op jit(solution)/shard_map/all_gather | solution.py:46
  323.3 0.0 copy-done.2
  323.3 15.2 %multiply_reduce_fusion = (f32[1536]{0:T(1024)S(1)}, f32[1536,704]{0,1:T(8,128)}) fusion(bf16[1,1536,704]{1,2,0:T(8,128)(2,1)S(1)} %copy-done.2, bf16[1536,4096]{1,0:T(8,128)(2,1)} %all-gather.2.cloned.1.call-done, bf16[1,704,4096]{2,1,0:T(8,128)(2,1)} %param.9), kind=kOutput, calls=%fused_computation.12 | convolution fusion | flops 8861612032 | bytes 24844288 | tf_op jit(solution)/shard_map/dot_general | solution.py:47
  338.4 0.1 all_to_all.15
  338.5 5.6 %psum.7 = f32[16,1,96]{2,1,0:T(1,128)} all-reduce(f32[16,1,96]{2,1,0:T(1,128)S(1)} %all_to_all.15), channel_id=1, replica_groups=mesh['expert'=16,'tensor'=2] {'tensor'}, use_global_device_ids=true, to_apply=%region_7.8 | all-reduce | flops 1536 | bytes 12288 | tf_op jit(solution)/shard_map/psum | solution.py:56
  344.1 5.6 %all-to-all-start.2 = ((f32[16,1,96]{2,1,0:T(1,128)}), f32[16,1,96]{2,1,0:T(1,128)S(1)}, u32[]{:S(2)}, u32[]{:S(2)}) async-start(f32[16,1,96]{2,1,0:T(1,128)} %psum.7), calls=%async_computation.2 | async-start | bytes 16384 | tf_op jit(solution)/shard_map/all_to_all | solution.py:57
  349.7 6.3 %all-to-all-done.2 = f32[16,1,96]{2,1,0:T(1,128)S(1)} async-done(((f32[16,1,96]{2,1,0:T(1,128)}), f32[16,1,96]{2,1,0:T(1,128)S(1)}, u32[]{:S(2)}, u32[]{:S(2)}) %all-to-all-start.2) | async-done | bytes 6176 | tf_op jit(solution)/shard_map/all_to_all | solution.py:57
  356.1 0.5 broadcast.90
  356.6 0.7 reduce.11
  357.3 0.1 reshape.107
  357.3 4.5 %gather_fusion.1 = f32[768]{0:T(1024)S(1)} fusion(f32[1536]{0:T(1024)S(1)} %reshape.107, s32[1024]{0:T(1024)S(1)} %pad_clamp_fusion.1), kind=kCustom, calls=%fused_computation.1 | custom fusion | bytes 9216 | tf_op jit(solution)/shard_map/gather | solution.py:60
  361.8 0.1 reshape.108
  361.9 0.1 copy.28
  362.1 0.1 copy.25
  362.2 0.1 reshape.130
  362.3 3.4 scatter_custom_fusion
  365.7 0.7 convert_element_type.61
  366.4 3.7 all-to-all-start
  370.1 0.6 fusion.13
  370.7 5.5 %all-to-all-done = bf16[16,1,96]{2,1,0:T(2,128)(2,1)S(1)} async-done(((bf16[16,1,96]{2,1,0:T(2,128)(2,1)}), bf16[16,1,96]{2,1,0:T(2,128)(2,1)S(1)}, u32[]{:S(2)}, u32[]{:S(2)}) %all-to-all-start) | async-done | bytes 3104 | tf_op jit(solution)/shard_map/all_to_all | solution.py:36
  376.2 0.1 reshape.109
  376.3 4.1 %fusion.6 = bf16[1,1536,704]{1,2,0:T(8,128)(2,1)} fusion(f32[1536,704]{0,1:T(8,128)} %get-tuple-element.12, f32[1536]{0:T(1024)S(1)} %reshape.109), kind=kLoop, calls=%fused_computation.14 | loop fusion | flops 2162688 | bytes 6494208 | tf_op jit(solution)/shard_map/broadcast_in_dim | solution.py:63
  380.4 14.0 %fusion.3 = bf16[1,704,4096]{2,1,0:T(8,128)(2,1)} fusion(bf16[1536,4096]{1,0:T(8,128)(2,1)} %all-gather.2.cloned.1.call-done, f32[1536]{0:T(1024)S(1)} %reshape.109, bf16[1,1536,704]{1,2,0:T(8,128)(2,1)S(1)} %copy-done.2), kind=kOutput, calls=%fused_computation.9 | convolution fusion | flops 8880128000 | bytes 20518912 | tf_op jit(solution)/shard_map/dot_general | solution.py:51
  (12 shorter events, 0.2 us)
Async XLA Ops:
  7.2 7.8 %copy-start = (bf16[128,2048]{1,0:T(8,128)(2,1)S(1)}, bf16[128,2048]{1,0:T(8,128)(2,1)}, u32[]{:S(2)}) copy-start(bf16[128,2048]{1,0:T(8,128)(2,1)} %param.5) | copy-start | bytes 1572868
  7.2 316.1 %all-gather.2.cloned.1.call-start = ((), (), s32[]{:S(2)}) async-start(), calls=%async_computation.3 | async-start | bytes 18874368 | tf_op jit(solution)/shard_map/all_gather | solution.py:46
  169.7 0.7 copy-start.1
  169.7 153.6 %copy-start.2 = (bf16[1,1536,704]{1,2,0:T(8,128)(2,1)S(1)}, bf16[1,1536,704]{1,2,0:T(8,128)(2,1)}, u32[]{:S(2)}) copy-start(bf16[1,1536,704]{1,2,0:T(8,128)(2,1)} %param.8) | copy-start | bytes 6488068
  344.1 12.0 %all-to-all-start.2 = ((f32[16,1,96]{2,1,0:T(1,128)}), f32[16,1,96]{2,1,0:T(1,128)S(1)}, u32[]{:S(2)}, u32[]{:S(2)}) async-start(f32[16,1,96]{2,1,0:T(1,128)} %psum.7), calls=%async_computation.2 | async-start | bytes 16384 | tf_op jit(solution)/shard_map/all_to_all | solution.py:57
  366.4 9.8 %all-to-all-start = ((bf16[16,1,96]{2,1,0:T(2,128)(2,1)}), bf16[16,1,96]{2,1,0:T(2,128)(2,1)S(1)}, u32[]{:S(2)}, u32[]{:S(2)}) async-start(bf16[16,1,96]{2,1,0:T(2,128)(2,1)} %convert_element_type.61), calls=%async_computation | async-start | bytes 16384 | tf_op jit(solution)/shard_map/all_to_all | solution.py:36
Sparse Core Ops, SparseCore 0:
  169.8 153.3 all-gather.1
where the time goes:
time: 402 us; the launch traced here: 401 us
  waiting for transfers between devices  165 us (41%)
  blocking collectives  150 us (37%)
  matrix products  29.2 us (7%)
  local copies, waits for them, and re-layouts  22.5 us (6%)
  between operations  14.2 us (4%)
  other arithmetic  11.3 us (3%)
  starting transfers between devices  9.31 us (2%)
    all_gather x1, waiting for transfers between devices, shards(): segment = lax.all_gather(narrow, 'tensor', axis=1, tiled=True)  153 us
    all_to_all x1, blocking collectives, shards(): lax.all_to_all(outgoing, 'expert', split_axis=0, concat_axis=0, tiled=True)  144 us
    dot_general x1, matrix products, shards(): lax.dot_general(segment, down_rows, (((1,), (1,)), ((), ())), preferred_e...  15.2 us
    dot_general x1, matrix products, shards(): lax.dot_general(saved_act, scaled, (((0,), (0,)), ((), ())), preferred_el...  14 us
  transfers between devices with their start and end apart: 3, of which 3 were waited for; matrix products, arithmetic and copies ran while one was open for 0% of the time, Pallas kernels for 0%

commit v1 on v0

--- a/solution.py
+++ b/solution.py
@@ -2,6 +2,22 @@
 import jax.numpy as jnp
 from jax import lax
 from jax.sharding import PartitionSpec as P
+
+
+def swapped_with_each(x, axis, split, join):
+    ways, here = (lax.axis_size(axis), lax.axis_index(axis))
+    width = x.shape[split] // ways
+    shape = list(x.shape)
+    shape[split] = width
+    height = shape[join]
+    shape[join] = height * ways
+    full = jnp.zeros(shape, x.dtype)
+    for mask in range(ways):
+        part = lax.dynamic_slice_in_dim(x, (here ^ mask) * width, width, axis=split)
+        if mask:
+            part = lax.ppermute(part, axis, [(d, d ^ mask) for d in range(ways)])
+        full = lax.dynamic_update_slice_in_dim(full, part, (here ^ mask) * height, axis=join)
+    return full
 
 
 def shards(grad_out, routes, scores, hidden_act, w_down):
@@ -32,7 +48,7 @@
         expert_count, per_source, -1
     )
     narrow, slot_weight = (
-        lax.all_to_all(outgoing, "expert", split_axis=0, concat_axis=0, tiled=True),
+        swapped_with_each(outgoing, "expert", 0, 0),
         lax.all_to_all(
             slot_probs.reshape(expert_count, per_source).astype(jnp.bfloat16),
             "expert",

time: 402 us -> 422 us (1.050)
  blocking collectives: 150 us -> 5.59 us
  waiting for transfers between devices: 165 us -> 257 us
  starting transfers between devices: 9.31 us -> 65.2 us
  local copies, waits for them, and re-layouts: 22.5 us -> 38.4 us
    all_to_all x1 -> x0, blocking collectives: 144 us -> none  [shards(): lax.all_to_all(outgoing, 'expert', split_axis=0, concat_axis=0, tiled=True)]
    ppermute x0 -> x15, waiting for transfers between devices: none -> 62.8 us  [swapped_with_each(): part = lax.ppermute(part, axis, [(d, d ^ mask) for d in range(ways)])]
    ppermute x0 -> x15, starting transfers between devices: none -> 56.1 us  [swapped_with_each(): part = lax.ppermute(part, axis, [(d, d ^ mask) for d in range(ways)])]
    all_gather x1, waiting for transfers between devices: 153 us -> 183 us  [shards(): segment = lax.all_gather(narrow, 'tensor', axis=1, tiled=True)]
    dynamic_update_slice x0 -> x15, local copies, waits for them, and re-layouts: none -> 11.7 us  [swapped_with_each(): lax.dynamic_update_slice_in_dim(full, part, (here ^ mask) * height, axis=...]
  transfers between devices with their start and end apart: 3 -> 18, of which waited for: 3 -> 9; matrix products, arithmetic and copies ran while one was open for 0% -> 3% of each run, Pallas kernels for 0% -> 0%
where the time goes in v1:
time: 422 us; the launch traced here: 421 us
  waiting for transfers between devices  257 us (61%)
  starting transfers between devices  65.2 us (15%)
  local copies, waits for them, and re-layouts  38.4 us (9%)
  matrix products  29.2 us (7%)
  between operations  14.3 us (3%)
  other arithmetic  11.3 us (3%)
  blocking collectives  5.59 us (1%)
    all_gather x1, waiting for transfers between devices, shards(): segment = lax.all_gather(narrow, 'tensor', axis=1, tiled=True)  183 us
    ppermute x15, waiting for transfers between devices, swapped_with_each(): part = lax.ppermute(part, axis, [(d, d ^ mask) for d in range(ways)])  62.8 us
    ppermute x15, starting transfers between devices, swapped_with_each(): part = lax.ppermute(part, axis, [(d, d ^ mask) for d in range(ways)])  56.1 us
    dot_general x1, matrix products, shards(): lax.dot_general(segment, down_rows, (((1,), (1,)), ((), ())), preferred_e...  15.2 us
    dot_general x1, matrix products, shards(): lax.dot_general(saved_act, scaled, (((0,), (0,)), ((), ())), preferred_el...  14 us
    dynamic_update_slice x15, local copies, waits for them, and re-layouts, swapped_with_each(): lax.dynamic_update_slice_in_dim(full, part, (here ^ mask) * height, axis=...  11.7 us
  transfers between devices with their start and end apart: 18, of which 9 were waited for; matrix products, arithmetic and copies ran while one was open for 3% of the time, Pallas kernels for 0%

profile of v1, /device:TPU:0, one launch (start us, length us, event | category | flops | bytes accessed | tf_op | source)
XLA Modules:
  0.0 421.5 jit_solution(2783977544367658436)
XLA Ops:
  7.3 0.8 copy.22
  8.1 0.1 eq.29
  8.3 0.1 eq.25
  8.4 0.7 broadcast_multiply_fusion
  9.1 1.7 reduce-window.6
  10.8 0.3 slice_reduce_fusion
  11.2 0.1 mul.49
  11.5 3.4 scatter_custom_fusion.1
  15.1 7.1 %gather_fusion = bf16[1536,2048]{1,0:T(8,128)(2,1)} fusion(bf16[128,2048]{1,0:T(8,128)(2,1)S(1)} %copy-done, s32[2048]{0:T(1024)S(1)} %pad_clamp_fusion), kind=kCustom, calls=%fused_computation | custom fusion | bytes 12589056 | tf_op jit(solution)/shard_map/jit(_take)/gather | solution.py:47
  22.1 3.3 broadcast_select_fusion
  25.4 3.4 broadcast_in_dim.34
  28.8 1.4 constant_dynamic-slice_fusion
  30.2 0.5 collective-permute-start
  30.7 2.5 collective-permute-start.1
  33.2 0.1 collective-permute-start.2
  33.3 1.8 collective-permute-start.3
  35.1 2.6 collective-permute-start.5
  37.7 0.8 constant_dynamic-update-slice_fusion.14
  38.5 4.7 %collective-permute-done.1 = bf16[1,96,2048]{2,1,0:T(8,128)(2,1)S(1)} collective-permute-done((bf16[1,96,2048]{2,1,0:T(8,128)(2,1)S(1)}, bf16[1,96,2048]{2,1,0:T(8,128)(2,1)S(1)}, u32[]{:S(2)}, u32[]{:S(2)}) %collective-permute-start.1) | collective-permute-done | bytes 393248 | tf_op jit(solution)/shard_map/ppermute | solution.py:18
  43.1 1.8 collective-permute-start.6
  44.9 0.8 constant_dynamic-update-slice_fusion.13
  45.7 5.5 %collective-permute-done.2 = bf16[1,96,2048]{2,1,0:T(8,128)(2,1)S(1)} collective-permute-done((bf16[1,96,2048]{2,1,0:T(8,128)(2,1)S(1)}, bf16[1,96,2048]{2,1,0:T(8,128)(2,1)S(1)}, u32[]{:S(2)}, u32[]{:S(2)}) %collective-permute-start.2) | collective-permute-done | bytes 393248 | tf_op jit(solution)/shard_map/ppermute | solution.py:18
  51.2 2.6 collective-permute-start.7
  53.7 0.8 constant_dynamic-update-slice_fusion.12
  54.5 0.2 collective-permute-start.8
  54.7 0.8 constant_dynamic-update-slice_fusion.11
  55.5 3.6 collective-permute-start.9
  59.1 0.8 constant_dynamic-update-slice_fusion.10
  59.9 20.4 %collective-permute-done.5 = bf16[1,96,2048]{2,1,0:T(8,128)(2,1)S(1)} collective-permute-done((bf16[1,96,2048]{2,1,0:T(8,128)(2,1)S(1)}, bf16[1,96,2048]{2,1,0:T(8,128)(2,1)S(1)}, u32[]{:S(2)}, u32[]{:S(2)}) %collective-permute-start.5) | collective-permute-done | bytes 393248 | tf_op jit(solution)/shard_map/ppermute | solution.py:18
  80.3 0.8 constant_dynamic-update-slice_fusion.9
  81.0 6.3 %collective-permute-done.6 = bf16[1,96,2048]{2,1,0:T(8,128)(2,1)S(1)} collective-permute-done((bf16[1,96,2048]{2,1,0:T(8,128)(2,1)S(1)}, bf16[1,96,2048]{2,1,0:T(8,128)(2,1)S(1)}, u32[]{:S(2)}, u32[]{:S(2)}) %collective-permute-start.6) | collective-permute-done | bytes 393248 | tf_op jit(solution)/shard_map/ppermute | solution.py:18
  87.3 1.3 collective-permute-start.11
  88.6 0.8 constant_dynamic-update-slice_fusion.8
  89.4 2.3 collective-permute-start.12
  91.8 0.8 constant_dynamic-update-slice_fusion.7
  92.6 34.3 %collective-permute-start.13 = (bf16[1,96,2048]{2,1,0:T(8,128)(2,1)S(1)}, bf16[1,96,2048]{2,1,0:T(8,128)(2,1)S(1)}, u32[]{:S(2)}, u32[]{:S(2)}) collective-permute-start(bf16[1,96,2048]{2,1,0:T(8,128)(2,1)S(1)} %get-tuple-element.12), channel_id=1, source_target_pairs={{0,28},{2,30},{4,24},{6,26},{8,20},{10,22},{12,16},{14,18},{16,12}... | collective-permute-start | bytes 1179656 | tf_op jit(solution)/shard_map/ppermute | solution.py:18
  126.8 0.8 constant_dynamic-update-slice_fusion.6
  127.6 13.2 %collective-permute-done.9 = bf16[1,96,2048]{2,1,0:T(8,128)(2,1)S(1)} collective-permute-done((bf16[1,96,2048]{2,1,0:T(8,128)(2,1)S(1)}, bf16[1,96,2048]{2,1,0:T(8,128)(2,1)S(1)}, u32[]{:S(2)}, u32[]{:S(2)}) %collective-permute-start.9) | collective-permute-done | bytes 393248 | tf_op jit(solution)/shard_map/ppermute | solution.py:18
  140.9 2.5 collective-permute-start.14
  143.4 0.8 constant_dynamic-update-slice_fusion.5
  144.2 12.8 %collective-permute-done.10 = bf16[1,96,2048]{2,1,0:T(8,128)(2,1)S(1)} collective-permute-done((bf16[1,96,2048]{2,1,0:T(8,128)(2,1)S(1)}, bf16[1,96,2048]{2,1,0:T(8,128)(2,1)S(1)}, u32[]{:S(2)}, u32[]{:S(2)}) %collective-permute-start.10) | collective-permute-done | bytes 393248 | tf_op jit(solution)/shard_map/ppermute | solution.py:18
  156.9 0.8 constant_dynamic-update-slice_fusion.4
  157.7 0.8 constant_dynamic-update-slice_fusion.3
  158.5 0.8 constant_dynamic-update-slice_fusion.2
  159.3 0.8 constant_dynamic-update-slice_fusion.1
  160.1 0.8 constant_dynamic-update-slice_fusion
  160.9 182.6 %all-gather.2.cloned.1.call-done = bf16[1536,4096]{1,0:T(8,128)(2,1)} async-done(((bf16[1536,2048]{1,0:T(8,128)(2,1)}), bf16[1536,4096]{1,0:T(8,128)(2,1)}) %all-gather.2.cloned.1.call-update) | async-done | bytes 12582928 | tf_op jit(solution)/shard_map/all_gather | solution.py:62
  343.5 15.2 %multiply_reduce_fusion = (f32[1536]{0:T(1024)S(1)}, f32[1536,704]{0,1:T(8,128)}) fusion(bf16[1,1536,704]{1,2,0:T(8,128)(2,1)S(1)} %copy-done.2, bf16[1536,4096]{1,0:T(8,128)(2,1)} %all-gather.2.cloned.1.call-done, bf16[1,704,4096]{2,1,0:T(8,128)(2,1)} %param.9), kind=kOutput, calls=%fused_computation.12 | convolution fusion | flops 8861612032 | bytes 24844288 | tf_op jit(solution)/shard_map/dot_general | solution.py:63
  358.8 5.6 %psum.7 = f32[16,1,96]{2,1,0:T(1,128)} all-reduce(f32[16,1,96]{2,1,0:T(1,128)S(1)} %all_to_all.11), channel_id=1, replica_groups=mesh['expert'=16,'tensor'=2] {'tensor'}, use_global_device_ids=true, to_apply=%region_7.8 | all-reduce | flops 1536 | bytes 12288 | tf_op jit(solution)/shard_map/psum | solution.py:72
  364.4 5.6 %all-to-all-start.1 = ((f32[16,1,96]{2,1,0:T(1,128)}), f32[16,1,96]{2,1,0:T(1,128)S(1)}, u32[]{:S(2)}, u32[]{:S(2)}) async-start(f32[16,1,96]{2,1,0:T(1,128)} %psum.7), calls=%async_computation.1 | async-start | bytes 16384 | tf_op jit(solution)/shard_map/all_to_all | solution.py:73
  370.0 6.3 %all-to-all-done.1 = f32[16,1,96]{2,1,0:T(1,128)S(1)} async-done(((f32[16,1,96]{2,1,0:T(1,128)}), f32[16,1,96]{2,1,0:T(1,128)S(1)}, u32[]{:S(2)}, u32[]{:S(2)}) %all-to-all-start.1) | async-done | bytes 6176 | tf_op jit(solution)/shard_map/all_to_all | solution.py:73
  376.4 0.5 broadcast.94
  376.9 0.7 reduce.11
  377.6 4.5 %gather_fusion.1 = f32[768]{0:T(1024)S(1)} fusion(f32[1536]{0:T(1024)S(1)} %reshape.107, s32[1024]{0:T(1024)S(1)} %pad_clamp_fusion.1), kind=kCustom, calls=%fused_computation.1 | custom fusion | bytes 9216 | tf_op jit(solution)/shard_map/gather | solution.py:76
  382.1 0.1 reshape.108
  382.3 0.1 copy.25
  382.4 0.1 reshape.130
  382.6 3.4 scatter_custom_fusion
  386.0 0.7 convert_element_type.61
  386.7 3.5 all-to-all-start
  390.1 0.6 fusion.13
  390.8 5.7 %all-to-all-done = bf16[16,1,96]{2,1,0:T(2,128)(2,1)S(1)} async-done(((bf16[16,1,96]{2,1,0:T(2,128)(2,1)}), bf16[16,1,96]{2,1,0:T(2,128)(2,1)S(1)}, u32[]{:S(2)}, u32[]{:S(2)}) %all-to-all-start) | async-done | bytes 3104 | tf_op jit(solution)/shard_map/all_to_all | solution.py:52
  396.6 4.1 fusion.6
  400.6 14.0 %fusion.3 = bf16[1,704,4096]{2,1,0:T(8,128)(2,1)} fusion(bf16[1536,4096]{1,0:T(8,128)(2,1)} %all-gather.2.cloned.1.call-done, f32[1536]{0:T(1024)S(1)} %reshape.109, bf16[1,1536,704]{1,2,0:T(8,128)(2,1)S(1)} %copy-done.2), kind=kOutput, calls=%fused_computation.9 | convolution fusion | flops 8880128000 | bytes 20518912 | tf_op jit(solution)/shard_map/dot_general | solution.py:67
  (38 shorter events, 0.9 us)
Async XLA Ops:
  7.2 7.9 %copy-start = (bf16[128,2048]{1,0:T(8,128)(2,1)S(1)}, bf16[128,2048]{1,0:T(8,128)(2,1)}, u32[]{:S(2)}) copy-start(bf16[128,2048]{1,0:T(8,128)(2,1)} %param.5) | copy-start | bytes 1572868
  7.2 336.3 %all-gather.2.cloned.1.call-start = ((), (), s32[]{:S(2)}) async-start(), calls=%async_computation.2 | async-start | bytes 18874368 | tf_op jit(solution)/shard_map/all_gather | solution.py:62
  30.2 4.9 %collective-permute-start = (bf16[1,96,2048]{2,1,0:T(8,128)(2,1)S(1)}, bf16[1,96,2048]{2,1,0:T(8,128)(2,1)S(1)}, u32[]{:S(2)}, u32[]{:S(2)}) collective-permute-start(bf16[1,96,2048]{2,1,0:T(8,128)(2,1)S(1)} %get-tuple-element.25), channel_id=1, source_target_pairs={{0,2},{2,0},{4,6},{6,4},{8,10},{10,8},{12,14},{14,12},{16,18},{18,... | collective-permute-start | bytes 1179656 | tf_op jit(solution)/shard_map/ppermute | solution.py:18
  30.7 12.4 %collective-permute-start.1 = (bf16[1,96,2048]{2,1,0:T(8,128)(2,1)S(1)}, bf16[1,96,2048]{2,1,0:T(8,128)(2,1)S(1)}, u32[]{:S(2)}, u32[]{:S(2)}) collective-permute-start(bf16[1,96,2048]{2,1,0:T(8,128)(2,1)S(1)} %get-tuple-element.24), channel_id=1, source_target_pairs={{0,4},{2,6},{4,0},{6,2},{8,12},{10,14},{12,8},{14,10},{16,20},{18,... | collective-permute-start | bytes 1179656 | tf_op jit(solution)/shard_map/ppermute | solution.py:18
  33.2 18.0 %collective-permute-start.2 = (bf16[1,96,2048]{2,1,0:T(8,128)(2,1)S(1)}, bf16[1,96,2048]{2,1,0:T(8,128)(2,1)S(1)}, u32[]{:S(2)}, u32[]{:S(2)}) collective-permute-start(bf16[1,96,2048]{2,1,0:T(8,128)(2,1)S(1)} %get-tuple-element.23), channel_id=1, source_target_pairs={{0,6},{2,4},{4,2},{6,0},{8,14},{10,12},{12,10},{14,8},{16,22},{18,... | collective-permute-start | bytes 1179656 | tf_op jit(solution)/shard_map/ppermute | solution.py:18
  33.3 21.2 %collective-permute-start.3 = (bf16[1,96,2048]{2,1,0:T(8,128)(2,1)S(1)}, bf16[1,96,2048]{2,1,0:T(8,128)(2,1)S(1)}, u32[]{:S(2)}, u32[]{:S(2)}) collective-permute-start(bf16[1,96,2048]{2,1,0:T(8,128)(2,1)S(1)} %get-tuple-element.22), channel_id=1, source_target_pairs={{0,8},{2,10},{4,12},{6,14},{8,0},{10,2},{12,4},{14,6},{16,24},{18,... | collective-permute-start | bytes 1179656 | tf_op jit(solution)/shard_map/ppermute | solution.py:18
  35.1 20.4 %collective-permute-start.4 = (bf16[1,96,2048]{2,1,0:T(8,128)(2,1)S(1)}, bf16[1,96,2048]{2,1,0:T(8,128)(2,1)S(1)}, u32[]{:S(2)}, u32[]{:S(2)}) collective-permute-start(bf16[1,96,2048]{2,1,0:T(8,128)(2,1)S(1)} %get-tuple-element.21), channel_id=1, source_target_pairs={{0,10},{2,8},{4,14},{6,12},{8,2},{10,0},{12,6},{14,4},{16,26},{18,... | collective-permute-start | bytes 1179656 | tf_op jit(solution)/shard_map/ppermute | solution.py:18
  35.1 45.2 %collective-permute-start.5 = (bf16[1,96,2048]{2,1,0:T(8,128)(2,1)S(1)}, bf16[1,96,2048]{2,1,0:T(8,128)(2,1)S(1)}, u32[]{:S(2)}, u32[]{:S(2)}) collective-permute-start(bf16[1,96,2048]{2,1,0:T(8,128)(2,1)S(1)} %get-tuple-element.20), channel_id=1, source_target_pairs={{0,12},{2,14},{4,8},{6,10},{8,4},{10,6},{12,0},{14,2},{16,28},{18,... | collective-permute-start | bytes 1179656 | tf_op jit(solution)/shard_map/ppermute | solution.py:18
  43.1 44.2 %collective-permute-start.6 = (bf16[1,96,2048]{2,1,0:T(8,128)(2,1)S(1)}, bf16[1,96,2048]{2,1,0:T(8,128)(2,1)S(1)}, u32[]{:S(2)}, u32[]{:S(2)}) collective-permute-start(bf16[1,96,2048]{2,1,0:T(8,128)(2,1)S(1)} %get-tuple-element.19), channel_id=1, source_target_pairs={{0,14},{2,12},{4,10},{6,8},{8,6},{10,4},{12,2},{14,0},{16,30},{18,... | collective-permute-start | bytes 1179656 | tf_op jit(solution)/shard_map/ppermute | solution.py:18
  51.2 38.2 %collective-permute-start.7 = (bf16[1,96,2048]{2,1,0:T(8,128)(2,1)S(1)}, bf16[1,96,2048]{2,1,0:T(8,128)(2,1)S(1)}, u32[]{:S(2)}, u32[]{:S(2)}) collective-permute-start(bf16[1,96,2048]{2,1,0:T(8,128)(2,1)S(1)} %get-tuple-element.18), channel_id=1, source_target_pairs={{0,16},{2,18},{4,20},{6,22},{8,24},{10,26},{12,28},{14,30},{16,0},... | collective-permute-start | bytes 1179656 | tf_op jit(solution)/shard_map/ppermute | solution.py:18
  54.5 38.0 %collective-permute-start.8 = (bf16[1,96,2048]{2,1,0:T(8,128)(2,1)S(1)}, bf16[1,96,2048]{2,1,0:T(8,128)(2,1)S(1)}, u32[]{:S(2)}, u32[]{:S(2)}) collective-permute-start(bf16[1,96,2048]{2,1,0:T(8,128)(2,1)S(1)} %get-tuple-element.17), channel_id=1, source_target_pairs={{0,18},{2,16},{4,22},{6,20},{8,26},{10,24},{12,30},{14,28},{16,2},... | collective-permute-start | bytes 1179656 | tf_op jit(solution)/shard_map/ppermute | solution.py:18
  55.5 85.4 %collective-permute-start.9 = (bf16[1,96,2048]{2,1,0:T(8,128)(2,1)S(1)}, bf16[1,96,2048]{2,1,0:T(8,128)(2,1)S(1)}, u32[]{:S(2)}, u32[]{:S(2)}) collective-permute-start(bf16[1,96,2048]{2,1,0:T(8,128)(2,1)S(1)} %get-tuple-element.16), channel_id=1, source_target_pairs={{0,20},{2,22},{4,16},{6,18},{8,28},{10,30},{12,24},{14,26},{16,4},... | collective-permute-start | bytes 1179656 | tf_op jit(solution)/shard_map/ppermute | solution.py:18
  80.3 76.7 %collective-permute-start.10 = (bf16[1,96,2048]{2,1,0:T(8,128)(2,1)S(1)}, bf16[1,96,2048]{2,1,0:T(8,128)(2,1)S(1)}, u32[]{:S(2)}, u32[]{:S(2)}) collective-permute-start(bf16[1,96,2048]{2,1,0:T(8,128)(2,1)S(1)} %get-tuple-element.15), channel_id=1, source_target_pairs={{0,22},{2,20},{4,18},{6,16},{8,30},{10,28},{12,26},{14,24},{16,6},... | collective-permute-start | bytes 1179656 | tf_op jit(solution)/shard_map/ppermute | solution.py:18
  87.3 70.4 %collective-permute-start.11 = (bf16[1,96,2048]{2,1,0:T(8,128)(2,1)S(1)}, bf16[1,96,2048]{2,1,0:T(8,128)(2,1)S(1)}, u32[]{:S(2)}, u32[]{:S(2)}) collective-permute-start(bf16[1,96,2048]{2,1,0:T(8,128)(2,1)S(1)} %get-tuple-element.14), channel_id=1, source_target_pairs={{0,24},{2,26},{4,28},{6,30},{8,16},{10,18},{12,20},{14,22},{16,8},... | collective-permute-start | bytes 1179656 | tf_op jit(solution)/shard_map/ppermute | solution.py:18
  89.4 71.5 %copy-start.1 = (f32[128,6]{0,1:T(8,128)S(1)}, f32[128,6]{0,1:T(8,128)}, u32[]{:S(2)}) copy-start(f32[128,6]{0,1:T(8,128)} %param.7) | copy-start | bytes 9220
  89.4 254.1 %copy-start.2 = (bf16[1,1536,704]{1,2,0:T(8,128)(2,1)S(1)}, bf16[1,1536,704]{1,2,0:T(8,128)(2,1)}, u32[]{:S(2)}) copy-start(bf16[1,1536,704]{1,2,0:T(8,128)(2,1)} %param.8) | copy-start | bytes 6488068
  89.4 69.1 %collective-permute-start.12 = (bf16[1,96,2048]{2,1,0:T(8,128)(2,1)S(1)}, bf16[1,96,2048]{2,1,0:T(8,128)(2,1)S(1)}, u32[]{:S(2)}, u32[]{:S(2)}) collective-permute-start(bf16[1,96,2048]{2,1,0:T(8,128)(2,1)S(1)} %get-tuple-element.13), channel_id=1, source_target_pairs={{0,26},{2,24},{4,30},{6,28},{8,18},{10,16},{12,22},{14,20},{16,10}... | collective-permute-start | bytes 1179656 | tf_op jit(solution)/shard_map/ppermute | solution.py:18
  92.6 66.7 %collective-permute-start.13 = (bf16[1,96,2048]{2,1,0:T(8,128)(2,1)S(1)}, bf16[1,96,2048]{2,1,0:T(8,128)(2,1)S(1)}, u32[]{:S(2)}, u32[]{:S(2)}) collective-permute-start(bf16[1,96,2048]{2,1,0:T(8,128)(2,1)S(1)} %get-tuple-element.12), channel_id=1, source_target_pairs={{0,28},{2,30},{4,24},{6,26},{8,20},{10,22},{12,16},{14,18},{16,12}... | collective-permute-start | bytes 1179656 | tf_op jit(solution)/shard_map/ppermute | solution.py:18
  140.9 19.2 %collective-permute-start.14 = (bf16[1,96,2048]{2,1,0:T(8,128)(2,1)S(1)}, bf16[1,96,2048]{2,1,0:T(8,128)(2,1)S(1)}, u32[]{:S(2)}, u32[]{:S(2)}) collective-permute-start(bf16[1,96,2048]{2,1,0:T(8,128)(2,1)S(1)} %get-tuple-element.11), channel_id=1, source_target_pairs={{0,30},{2,28},{4,26},{6,24},{8,22},{10,20},{12,18},{14,16},{16,14}... | collective-permute-start | bytes 1179656 | tf_op jit(solution)/shard_map/ppermute | solution.py:18
  364.4 12.0 %all-to-all-start.1 = ((f32[16,1,96]{2,1,0:T(1,128)}), f32[16,1,96]{2,1,0:T(1,128)S(1)}, u32[]{:S(2)}, u32[]{:S(2)}) async-start(f32[16,1,96]{2,1,0:T(1,128)} %psum.7), calls=%async_computation.1 | async-start | bytes 16384 | tf_op jit(solution)/shard_map/all_to_all | solution.py:73
  386.7 9.8 %all-to-all-start = ((bf16[16,1,96]{2,1,0:T(2,128)(2,1)}), bf16[16,1,96]{2,1,0:T(2,128)(2,1)S(1)}, u32[]{:S(2)}, u32[]{:S(2)}) async-start(bf16[16,1,96]{2,1,0:T(2,128)(2,1)} %convert_element_type.61), calls=%async_computation | async-start | bytes 16384 | tf_op jit(solution)/shard_map/all_to_all | solution.py:52
Sparse Core Ops, SparseCore 0:
  161.0 182.4 all-gather.1
